TPU v7x, 128 devices: a whole 4x4x4 slice. The times are simulated.
128 devices in a mesh: grp: 4 (over y), row: 32 (over x, z, core).
Axes of the slice: x: 4, y: 4, z: 4, core: 2. Of those that a mesh axis runs over, the one named last changes fastest.
Arguments:
- b_tensor: bfloat16 [9984, 8, 768], P(None, 'grp', 'row'), may hold values from -0.21875 to 0.21875
- aux_counts: int32 [4], replicated, may hold values from 1 to 2, as said below
Outputs:
- exchange_matrix: float32 [9984, 9984], P('row', 'grp')
Inputs may be any that keep to these rules, and one draw needn't show every extreme that they name: `aux_counts`: some group has all 2 slots live.
All inputs are finite; a program needn't handle non-finite values.
Results may differ from a plain program's by a relative error of at most 0.0003.
Values may be sent and summed in bfloat16 or wider, within the bound.
No kernel may reach another device: no remote copies, remote signals or barrier semaphores. Data moves between devices by JAX's collectives and lax.ppermute only.
A program may use at most 128 MiB of HBM per device.

v0:
```python
import jax
import jax.numpy as jnp
from jax import lax
from jax.sharding import PartitionSpec as P


def shifted(block, axis, distance):
    devices = range(lax.axis_size(axis))
    route = [((i - distance) % len(devices), i) for i in devices]
    return lax.ppermute(block, axis, route)


def shards(b_tensor, aux_counts):
    row_count = lax.axis_size("row")
    row_rank = lax.axis_index("row")
    group_index = lax.axis_index("grp")
    slot_count = b_tensor.shape[1]
    live_count = lax.dynamic_index_in_dim(aux_counts, group_index, 0, keepdims=False)
    live_mask = (jnp.arange(slot_count) < live_count).astype(jnp.bfloat16)
    masked = b_tensor * live_mask[None, :, None]
    regrouped = lax.all_to_all(masked, "row", split_axis=0, concat_axis=2, tiled=True)
    block_size = regrouped.shape[0]
    own_rows = regrouped.reshape(block_size, -1)

    def tile_with(visitor):
        return lax.dot_general(
            own_rows, visitor, (((1,), (1,)), ((), ())), preferred_element_type=jnp.float32
        )

    upper_part = jnp.zeros((block_size, row_count, block_size), jnp.float32)
    upper_part = lax.dynamic_update_index_in_dim(upper_part, tile_with(own_rows), row_rank, 1)

    def advance(cycle_step, state_tuple):
        visiting, upper_acc = state_tuple
        visiting = shifted(visiting, "row", -1)
        target = (row_rank + cycle_step) % row_count
        upper_acc = lax.dynamic_update_index_in_dim(upper_acc, tile_with(visiting), target, 1)
        return (visiting, upper_acc)

    visiting, upper_part = lax.fori_loop(1, row_count, advance, (own_rows, upper_part))
    partial_value = upper_part.reshape(block_size, row_count * block_size)
    return lax.psum_scatter(partial_value, "grp", scatter_dimension=1, tiled=True)


def solution(mesh):
    return jax.shard_map(
        shards,
        mesh=mesh,
        in_specs=(P(None, "grp", "row"), P()),
        out_specs=P("row", "grp"),
        check_vma=False,
    )
```

profile of v0, /device:TPU:1, one launch (start us, length us, event | category | flops | bytes accessed | tf_op | source)
XLA Modules:
  0.0 851.2 jit_solution(9750454119854476417)
XLA Ops:
  17.7 16.5 %reshape.17 = bf16[32,2,7488]{2,1,0:T(2,128)(2,1)} reshape(bf16[9984,2,24]{2,1,0:T(2,128)(2,1)} %copy.14) | data formatting | bytes 1916928
  43.7 16.0 %all-to-all-done = bf16[32,2,7488]{2,1,0:T(2,128)(2,1)S(1)} async-done(((bf16[32,2,7488]{2,1,0:T(2,128)(2,1)}), bf16[32,2,7488]{2,1,0:T(2,128)(2,1)S(1)}, u32[]{:S(2)}, u32[]{:S(2)}) %all-to-all-start) | async-done | bytes 958496 | tf_op jit(solution)/shard_map/all_to_all | solution.py:21
  92.7 577.8 %while.17 = (s32[]{:T(128)}, bf16[312,1536]{1,0:T(8,128)(2,1)}, f32[312,32,312]{2,0,1:T(8,128)}, bf16[312,1536]{1,0:T(8,128)(2,1)S(1)}, s32[]{:T(128)}, /*index=5*/s32[]{:T(128)}, s32[]{:T(128)}, s32[]{:T(128)}, s32[]{:T(128)}) while((s32[]{:T(128)}, bf16[312,1536]{1,0:T(8,128)(2,1)}, f32[312,32,312]{2,0,1:T(8,128)}, ...), condition=%wide.region_1.2_spmd, body=%wide.region_0.1_spmd.sunk | while | flops 299040768 | bytes 8147236 | solution.py:40
  92.8 13.4 %collective-permute-done = bf16[312,1536]{1,0:T(8,128)(2,1)S(1)} collective-permute-done((bf16[312,1536]{1,0:T(8,128)(2,1)}, bf16[312,1536]{1,0:T(8,128)(2,1)S(1)}, u32[]{:S(2)}, u32[]{:S(2)}) %collective-permute-start) | collective-permute-done | bytes 958496 | tf_op jit(solution)/shard_map/while/body/eval_jaxpr/ppermute | solution.py:10
  172.1 13.6 %collective-permute-start = (bf16[312,1536]{1,0:T(8,128)(2,1)}, bf16[312,1536]{1,0:T(8,128)(2,1)S(1)}, u32[]{:S(2)}, u32[]{:S(2)}) collective-permute-start(bf16[312,1536]{1,0:T(8,128)(2,1)} %get-tuple-element.205), channel_id=1, source_target_pairs={{1,0},{2,1},{3,2},{4,3},{5,4},{6,5},{7,6},{8,7},{9,8},{10,9},{11,1... | collective-permute-start | bytes 2875400 | tf_op jit(solution)/shard_map/while/body/eval_jaxpr/ppermute | solution.py:10
  190.5 14.5 %collective-permute-start = (bf16[312,1536]{1,0:T(8,128)(2,1)}, bf16[312,1536]{1,0:T(8,128)(2,1)S(1)}, u32[]{:S(2)}, u32[]{:S(2)}) collective-permute-start(bf16[312,1536]{1,0:T(8,128)(2,1)} %get-tuple-element.205), channel_id=1, source_target_pairs={{1,0},{2,1},{3,2},{4,3},{5,4},{6,5},{7,6},{8,7},{9,8},{10,9},{11,1... | collective-permute-start | bytes 2875400 | tf_op jit(solution)/shard_map/while/body/eval_jaxpr/ppermute | solution.py:10
  209.7 14.4 %collective-permute-start = (bf16[312,1536]{1,0:T(8,128)(2,1)}, bf16[312,1536]{1,0:T(8,128)(2,1)S(1)}, u32[]{:S(2)}, u32[]{:S(2)}) collective-permute-start(bf16[312,1536]{1,0:T(8,128)(2,1)} %get-tuple-element.205), channel_id=1, source_target_pairs={{1,0},{2,1},{3,2},{4,3},{5,4},{6,5},{7,6},{8,7},{9,8},{10,9},{11,1... | collective-permute-start | bytes 2875400 | tf_op jit(solution)/shard_map/while/body/eval_jaxpr/ppermute | solution.py:10
  228.9 14.4 %collective-permute-start = (bf16[312,1536]{1,0:T(8,128)(2,1)}, bf16[312,1536]{1,0:T(8,128)(2,1)S(1)}, u32[]{:S(2)}, u32[]{:S(2)}) collective-permute-start(bf16[312,1536]{1,0:T(8,128)(2,1)} %get-tuple-element.205), channel_id=1, source_target_pairs={{1,0},{2,1},{3,2},{4,3},{5,4},{6,5},{7,6},{8,7},{9,8},{10,9},{11,1... | collective-permute-start | bytes 2875400 | tf_op jit(solution)/shard_map/while/body/eval_jaxpr/ppermute | solution.py:10
  248.1 14.4 %collective-permute-start = (bf16[312,1536]{1,0:T(8,128)(2,1)}, bf16[312,1536]{1,0:T(8,128)(2,1)S(1)}, u32[]{:S(2)}, u32[]{:S(2)}) collective-permute-start(bf16[312,1536]{1,0:T(8,128)(2,1)} %get-tuple-element.205), channel_id=1, source_target_pairs={{1,0},{2,1},{3,2},{4,3},{5,4},{6,5},{7,6},{8,7},{9,8},{10,9},{11,1... | collective-permute-start | bytes 2875400 | tf_op jit(solution)/shard_map/while/body/eval_jaxpr/ppermute | solution.py:10
  267.3 14.4 %collective-permute-start = (bf16[312,1536]{1,0:T(8,128)(2,1)}, bf16[312,1536]{1,0:T(8,128)(2,1)S(1)}, u32[]{:S(2)}, u32[]{:S(2)}) collective-permute-start(bf16[312,1536]{1,0:T(8,128)(2,1)} %get-tuple-element.205), channel_id=1, source_target_pairs={{1,0},{2,1},{3,2},{4,3},{5,4},{6,5},{7,6},{8,7},{9,8},{10,9},{11,1... | collective-permute-start | bytes 2875400 | tf_op jit(solution)/shard_map/while/body/eval_jaxpr/ppermute | solution.py:10
  286.4 14.5 %collective-permute-start = (bf16[312,1536]{1,0:T(8,128)(2,1)}, bf16[312,1536]{1,0:T(8,128)(2,1)S(1)}, u32[]{:S(2)}, u32[]{:S(2)}) collective-permute-start(bf16[312,1536]{1,0:T(8,128)(2,1)} %get-tuple-element.205), channel_id=1, source_target_pairs={{1,0},{2,1},{3,2},{4,3},{5,4},{6,5},{7,6},{8,7},{9,8},{10,9},{11,1... | collective-permute-start | bytes 2875400 | tf_op jit(solution)/shard_map/while/body/eval_jaxpr/ppermute | solution.py:10
  305.7 14.4 %collective-permute-start = (bf16[312,1536]{1,0:T(8,128)(2,1)}, bf16[312,1536]{1,0:T(8,128)(2,1)S(1)}, u32[]{:S(2)}, u32[]{:S(2)}) collective-permute-start(bf16[312,1536]{1,0:T(8,128)(2,1)} %get-tuple-element.205), channel_id=1, source_target_pairs={{1,0},{2,1},{3,2},{4,3},{5,4},{6,5},{7,6},{8,7},{9,8},{10,9},{11,1... | collective-permute-start | bytes 2875400 | tf_op jit(solution)/shard_map/while/body/eval_jaxpr/ppermute | solution.py:10
  324.9 14.4 %collective-permute-start = (bf16[312,1536]{1,0:T(8,128)(2,1)}, bf16[312,1536]{1,0:T(8,128)(2,1)S(1)}, u32[]{:S(2)}, u32[]{:S(2)}) collective-permute-start(bf16[312,1536]{1,0:T(8,128)(2,1)} %get-tuple-element.205), channel_id=1, source_target_pairs={{1,0},{2,1},{3,2},{4,3},{5,4},{6,5},{7,6},{8,7},{9,8},{10,9},{11,1... | collective-permute-start | bytes 2875400 | tf_op jit(solution)/shard_map/while/body/eval_jaxpr/ppermute | solution.py:10
  344.1 14.4 %collective-permute-start = (bf16[312,1536]{1,0:T(8,128)(2,1)}, bf16[312,1536]{1,0:T(8,128)(2,1)S(1)}, u32[]{:S(2)}, u32[]{:S(2)}) collective-permute-start(bf16[312,1536]{1,0:T(8,128)(2,1)} %get-tuple-element.205), channel_id=1, source_target_pairs={{1,0},{2,1},{3,2},{4,3},{5,4},{6,5},{7,6},{8,7},{9,8},{10,9},{11,1... | collective-permute-start | bytes 2875400 | tf_op jit(solution)/shard_map/while/body/eval_jaxpr/ppermute | solution.py:10
  363.2 14.4 %collective-permute-start = (bf16[312,1536]{1,0:T(8,128)(2,1)}, bf16[312,1536]{1,0:T(8,128)(2,1)S(1)}, u32[]{:S(2)}, u32[]{:S(2)}) collective-permute-start(bf16[312,1536]{1,0:T(8,128)(2,1)} %get-tuple-element.205), channel_id=1, source_target_pairs={{1,0},{2,1},{3,2},{4,3},{5,4},{6,5},{7,6},{8,7},{9,8},{10,9},{11,1... | collective-permute-start | bytes 2875400 | tf_op jit(solution)/shard_map/while/body/eval_jaxpr/ppermute | solution.py:10
  382.5 14.4 %collective-permute-start = (bf16[312,1536]{1,0:T(8,128)(2,1)}, bf16[312,1536]{1,0:T(8,128)(2,1)S(1)}, u32[]{:S(2)}, u32[]{:S(2)}) collective-permute-start(bf16[312,1536]{1,0:T(8,128)(2,1)} %get-tuple-element.205), channel_id=1, source_target_pairs={{1,0},{2,1},{3,2},{4,3},{5,4},{6,5},{7,6},{8,7},{9,8},{10,9},{11,1... | collective-permute-start | bytes 2875400 | tf_op jit(solution)/shard_map/while/body/eval_jaxpr/ppermute | solution.py:10
  401.7 14.4 %collective-permute-start = (bf16[312,1536]{1,0:T(8,128)(2,1)}, bf16[312,1536]{1,0:T(8,128)(2,1)S(1)}, u32[]{:S(2)}, u32[]{:S(2)}) collective-permute-start(bf16[312,1536]{1,0:T(8,128)(2,1)} %get-tuple-element.205), channel_id=1, source_target_pairs={{1,0},{2,1},{3,2},{4,3},{5,4},{6,5},{7,6},{8,7},{9,8},{10,9},{11,1... | collective-permute-start | bytes 2875400 | tf_op jit(solution)/shard_map/while/body/eval_jaxpr/ppermute | solution.py:10
  420.9 14.4 %collective-permute-start = (bf16[312,1536]{1,0:T(8,128)(2,1)}, bf16[312,1536]{1,0:T(8,128)(2,1)S(1)}, u32[]{:S(2)}, u32[]{:S(2)}) collective-permute-start(bf16[312,1536]{1,0:T(8,128)(2,1)} %get-tuple-element.205), channel_id=1, source_target_pairs={{1,0},{2,1},{3,2},{4,3},{5,4},{6,5},{7,6},{8,7},{9,8},{10,9},{11,1... | collective-permute-start | bytes 2875400 | tf_op jit(solution)/shard_map/while/body/eval_jaxpr/ppermute | solution.py:10
  440.1 14.4 %collective-permute-start = (bf16[312,1536]{1,0:T(8,128)(2,1)}, bf16[312,1536]{1,0:T(8,128)(2,1)S(1)}, u32[]{:S(2)}, u32[]{:S(2)}) collective-permute-start(bf16[312,1536]{1,0:T(8,128)(2,1)} %get-tuple-element.205), channel_id=1, source_target_pairs={{1,0},{2,1},{3,2},{4,3},{5,4},{6,5},{7,6},{8,7},{9,8},{10,9},{11,1... | collective-permute-start | bytes 2875400 | tf_op jit(solution)/shard_map/while/body/eval_jaxpr/ppermute | solution.py:10
  459.3 14.5 %collective-permute-start = (bf16[312,1536]{1,0:T(8,128)(2,1)}, bf16[312,1536]{1,0:T(8,128)(2,1)S(1)}, u32[]{:S(2)}, u32[]{:S(2)}) collective-permute-start(bf16[312,1536]{1,0:T(8,128)(2,1)} %get-tuple-element.205), channel_id=1, source_target_pairs={{1,0},{2,1},{3,2},{4,3},{5,4},{6,5},{7,6},{8,7},{9,8},{10,9},{11,1... | collective-permute-start | bytes 2875400 | tf_op jit(solution)/shard_map/while/body/eval_jaxpr/ppermute | solution.py:10
  478.5 14.4 %collective-permute-start = (bf16[312,1536]{1,0:T(8,128)(2,1)}, bf16[312,1536]{1,0:T(8,128)(2,1)S(1)}, u32[]{:S(2)}, u32[]{:S(2)}) collective-permute-start(bf16[312,1536]{1,0:T(8,128)(2,1)} %get-tuple-element.205), channel_id=1, source_target_pairs={{1,0},{2,1},{3,2},{4,3},{5,4},{6,5},{7,6},{8,7},{9,8},{10,9},{11,1... | collective-permute-start | bytes 2875400 | tf_op jit(solution)/shard_map/while/body/eval_jaxpr/ppermute | solution.py:10
  497.7 14.5 %collective-permute-start = (bf16[312,1536]{1,0:T(8,128)(2,1)}, bf16[312,1536]{1,0:T(8,128)(2,1)S(1)}, u32[]{:S(2)}, u32[]{:S(2)}) collective-permute-start(bf16[312,1536]{1,0:T(8,128)(2,1)} %get-tuple-element.205), channel_id=1, source_target_pairs={{1,0},{2,1},{3,2},{4,3},{5,4},{6,5},{7,6},{8,7},{9,8},{10,9},{11,1... | collective-permute-start | bytes 2875400 | tf_op jit(solution)/shard_map/while/body/eval_jaxpr/ppermute | solution.py:10
  516.9 14.4 %collective-permute-start = (bf16[312,1536]{1,0:T(8,128)(2,1)}, bf16[312,1536]{1,0:T(8,128)(2,1)S(1)}, u32[]{:S(2)}, u32[]{:S(2)}) collective-permute-start(bf16[312,1536]{1,0:T(8,128)(2,1)} %get-tuple-element.205), channel_id=1, source_target_pairs={{1,0},{2,1},{3,2},{4,3},{5,4},{6,5},{7,6},{8,7},{9,8},{10,9},{11,1... | collective-permute-start | bytes 2875400 | tf_op jit(solution)/shard_map/while/body/eval_jaxpr/ppermute | solution.py:10
  536.1 14.4 %collective-permute-start = (bf16[312,1536]{1,0:T(8,128)(2,1)}, bf16[312,1536]{1,0:T(8,128)(2,1)S(1)}, u32[]{:S(2)}, u32[]{:S(2)}) collective-permute-start(bf16[312,1536]{1,0:T(8,128)(2,1)} %get-tuple-element.205), channel_id=1, source_target_pairs={{1,0},{2,1},{3,2},{4,3},{5,4},{6,5},{7,6},{8,7},{9,8},{10,9},{11,1... | collective-permute-start | bytes 2875400 | tf_op jit(solution)/shard_map/while/body/eval_jaxpr/ppermute | solution.py:10
  555.3 14.4 %collective-permute-start = (bf16[312,1536]{1,0:T(8,128)(2,1)}, bf16[312,1536]{1,0:T(8,128)(2,1)S(1)}, u32[]{:S(2)}, u32[]{:S(2)}) collective-permute-start(bf16[312,1536]{1,0:T(8,128)(2,1)} %get-tuple-element.205), channel_id=1, source_target_pairs={{1,0},{2,1},{3,2},{4,3},{5,4},{6,5},{7,6},{8,7},{9,8},{10,9},{11,1... | collective-permute-start | bytes 2875400 | tf_op jit(solution)/shard_map/while/body/eval_jaxpr/ppermute | solution.py:10
  574.6 14.4 %collective-permute-start = (bf16[312,1536]{1,0:T(8,128)(2,1)}, bf16[312,1536]{1,0:T(8,128)(2,1)S(1)}, u32[]{:S(2)}, u32[]{:S(2)}) collective-permute-start(bf16[312,1536]{1,0:T(8,128)(2,1)} %get-tuple-element.205), channel_id=1, source_target_pairs={{1,0},{2,1},{3,2},{4,3},{5,4},{6,5},{7,6},{8,7},{9,8},{10,9},{11,1... | collective-permute-start | bytes 2875400 | tf_op jit(solution)/shard_map/while/body/eval_jaxpr/ppermute | solution.py:10
  593.7 14.5 %collective-permute-start = (bf16[312,1536]{1,0:T(8,128)(2,1)}, bf16[312,1536]{1,0:T(8,128)(2,1)S(1)}, u32[]{:S(2)}, u32[]{:S(2)}) collective-permute-start(bf16[312,1536]{1,0:T(8,128)(2,1)} %get-tuple-element.205), channel_id=1, source_target_pairs={{1,0},{2,1},{3,2},{4,3},{5,4},{6,5},{7,6},{8,7},{9,8},{10,9},{11,1... | collective-permute-start | bytes 2875400 | tf_op jit(solution)/shard_map/while/body/eval_jaxpr/ppermute | solution.py:10
  612.9 14.4 %collective-permute-start = (bf16[312,1536]{1,0:T(8,128)(2,1)}, bf16[312,1536]{1,0:T(8,128)(2,1)S(1)}, u32[]{:S(2)}, u32[]{:S(2)}) collective-permute-start(bf16[312,1536]{1,0:T(8,128)(2,1)} %get-tuple-element.205), channel_id=1, source_target_pairs={{1,0},{2,1},{3,2},{4,3},{5,4},{6,5},{7,6},{8,7},{9,8},{10,9},{11,1... | collective-permute-start | bytes 2875400 | tf_op jit(solution)/shard_map/while/body/eval_jaxpr/ppermute | solution.py:10
  632.1 14.5 %collective-permute-start = (bf16[312,1536]{1,0:T(8,128)(2,1)}, bf16[312,1536]{1,0:T(8,128)(2,1)S(1)}, u32[]{:S(2)}, u32[]{:S(2)}) collective-permute-start(bf16[312,1536]{1,0:T(8,128)(2,1)} %get-tuple-element.205), channel_id=1, source_target_pairs={{1,0},{2,1},{3,2},{4,3},{5,4},{6,5},{7,6},{8,7},{9,8},{10,9},{11,1... | collective-permute-start | bytes 2875400 | tf_op jit(solution)/shard_map/while/body/eval_jaxpr/ppermute | solution.py:10
  651.3 14.4 %collective-permute-start = (bf16[312,1536]{1,0:T(8,128)(2,1)}, bf16[312,1536]{1,0:T(8,128)(2,1)S(1)}, u32[]{:S(2)}, u32[]{:S(2)}) collective-permute-start(bf16[312,1536]{1,0:T(8,128)(2,1)} %get-tuple-element.205), channel_id=1, source_target_pairs={{1,0},{2,1},{3,2},{4,3},{5,4},{6,5},{7,6},{8,7},{9,8},{10,9},{11,1... | collective-permute-start | bytes 2875400 | tf_op jit(solution)/shard_map/while/body/eval_jaxpr/ppermute | solution.py:10
  670.5 16.9 %copy.25 = f32[312,32,312]{0,2,1:T(8,128)} copy(f32[312,32,312]{2,0,1:T(8,128)} %get-tuple-element.138) | data formatting | bytes 24920064
  687.5 151.8 %reduce-scatter.4.cloned.1.call-done = f32[2496,312]{1,0:T(8,128)} async-done(((f32[9984,312]{1,0:T(8,128)}), f32[2496,312]{1,0:T(8,128)}) %reduce-scatter.4.cloned.1.call-update) | async-done | bytes 3115024
  (114 shorter events, 248.9 us)
Async XLA Ops:
  34.2 25.5 %all-to-all-start = ((bf16[32,2,7488]{2,1,0:T(2,128)(2,1)}), bf16[32,2,7488]{2,1,0:T(2,128)(2,1)S(1)}, u32[]{:S(2)}, u32[]{:S(2)}) async-start(bf16[32,2,7488]{2,1,0:T(2,128)(2,1)} %reshape.17), calls=%async_computation | async-start | bytes 1933312 | tf_op jit(solution)/shard_map/all_to_all | solution.py:21
  43.6 795.6 %reduce-scatter.4.cloned.1.call-start = ((), (), s32[]{:S(2)}) async-start(), calls=%async_computation.2 | async-start | bytes 19169280
  92.7 13.5 %collective-permute-start = (bf16[312,1536]{1,0:T(8,128)(2,1)}, bf16[312,1536]{1,0:T(8,128)(2,1)S(1)}, u32[]{:S(2)}, u32[]{:S(2)}) collective-permute-start(bf16[312,1536]{1,0:T(8,128)(2,1)} %get-tuple-element.205), channel_id=1, source_target_pairs={{1,0},{2,1},{3,2},{4,3},{5,4},{6,5},{7,6},{8,7},{9,8},{10,9},{11,1... | collective-permute-start | bytes 2875400 | tf_op jit(solution)/shard_map/while/body/eval_jaxpr/ppermute | solution.py:10
  108.6 13.5 %collective-permute-start = (bf16[312,1536]{1,0:T(8,128)(2,1)}, bf16[312,1536]{1,0:T(8,128)(2,1)S(1)}, u32[]{:S(2)}, u32[]{:S(2)}) collective-permute-start(bf16[312,1536]{1,0:T(8,128)(2,1)} %get-tuple-element.205), channel_id=1, source_target_pairs={{1,0},{2,1},{3,2},{4,3},{5,4},{6,5},{7,6},{8,7},{9,8},{10,9},{11,1... | collective-permute-start | bytes 2875400 | tf_op jit(solution)/shard_map/while/body/eval_jaxpr/ppermute | solution.py:10
  124.5 13.5 %collective-permute-start = (bf16[312,1536]{1,0:T(8,128)(2,1)}, bf16[312,1536]{1,0:T(8,128)(2,1)S(1)}, u32[]{:S(2)}, u32[]{:S(2)}) collective-permute-start(bf16[312,1536]{1,0:T(8,128)(2,1)} %get-tuple-element.205), channel_id=1, source_target_pairs={{1,0},{2,1},{3,2},{4,3},{5,4},{6,5},{7,6},{8,7},{9,8},{10,9},{11,1... | collective-permute-start | bytes 2875400 | tf_op jit(solution)/shard_map/while/body/eval_jaxpr/ppermute | solution.py:10
  156.2 13.5 %collective-permute-start = (bf16[312,1536]{1,0:T(8,128)(2,1)}, bf16[312,1536]{1,0:T(8,128)(2,1)S(1)}, u32[]{:S(2)}, u32[]{:S(2)}) collective-permute-start(bf16[312,1536]{1,0:T(8,128)(2,1)} %get-tuple-element.205), channel_id=1, source_target_pairs={{1,0},{2,1},{3,2},{4,3},{5,4},{6,5},{7,6},{8,7},{9,8},{10,9},{11,1... | collective-permute-start | bytes 2875400 | tf_op jit(solution)/shard_map/while/body/eval_jaxpr/ppermute | solution.py:10
  172.1 16.0 %collective-permute-start = (bf16[312,1536]{1,0:T(8,128)(2,1)}, bf16[312,1536]{1,0:T(8,128)(2,1)S(1)}, u32[]{:S(2)}, u32[]{:S(2)}) collective-permute-start(bf16[312,1536]{1,0:T(8,128)(2,1)} %get-tuple-element.205), channel_id=1, source_target_pairs={{1,0},{2,1},{3,2},{4,3},{5,4},{6,5},{7,6},{8,7},{9,8},{10,9},{11,1... | collective-permute-start | bytes 2875400 | tf_op jit(solution)/shard_map/while/body/eval_jaxpr/ppermute | solution.py:10
  190.5 16.8 %collective-permute-start = (bf16[312,1536]{1,0:T(8,128)(2,1)}, bf16[312,1536]{1,0:T(8,128)(2,1)S(1)}, u32[]{:S(2)}, u32[]{:S(2)}) collective-permute-start(bf16[312,1536]{1,0:T(8,128)(2,1)} %get-tuple-element.205), channel_id=1, source_target_pairs={{1,0},{2,1},{3,2},{4,3},{5,4},{6,5},{7,6},{8,7},{9,8},{10,9},{11,1... | collective-permute-start | bytes 2875400 | tf_op jit(solution)/shard_map/while/body/eval_jaxpr/ppermute | solution.py:10
  209.7 16.8 %collective-permute-start = (bf16[312,1536]{1,0:T(8,128)(2,1)}, bf16[312,1536]{1,0:T(8,128)(2,1)S(1)}, u32[]{:S(2)}, u32[]{:S(2)}) collective-permute-start(bf16[312,1536]{1,0:T(8,128)(2,1)} %get-tuple-element.205), channel_id=1, source_target_pairs={{1,0},{2,1},{3,2},{4,3},{5,4},{6,5},{7,6},{8,7},{9,8},{10,9},{11,1... | collective-permute-start | bytes 2875400 | tf_op jit(solution)/shard_map/while/body/eval_jaxpr/ppermute | solution.py:10
  228.9 16.8 %collective-permute-start = (bf16[312,1536]{1,0:T(8,128)(2,1)}, bf16[312,1536]{1,0:T(8,128)(2,1)S(1)}, u32[]{:S(2)}, u32[]{:S(2)}) collective-permute-start(bf16[312,1536]{1,0:T(8,128)(2,1)} %get-tuple-element.205), channel_id=1, source_target_pairs={{1,0},{2,1},{3,2},{4,3},{5,4},{6,5},{7,6},{8,7},{9,8},{10,9},{11,1... | collective-permute-start | bytes 2875400 | tf_op jit(solution)/shard_map/while/body/eval_jaxpr/ppermute | solution.py:10
  248.1 16.8 %collective-permute-start = (bf16[312,1536]{1,0:T(8,128)(2,1)}, bf16[312,1536]{1,0:T(8,128)(2,1)S(1)}, u32[]{:S(2)}, u32[]{:S(2)}) collective-permute-start(bf16[312,1536]{1,0:T(8,128)(2,1)} %get-tuple-element.205), channel_id=1, source_target_pairs={{1,0},{2,1},{3,2},{4,3},{5,4},{6,5},{7,6},{8,7},{9,8},{10,9},{11,1... | collective-permute-start | bytes 2875400 | tf_op jit(solution)/shard_map/while/body/eval_jaxpr/ppermute | solution.py:10
  267.3 16.8 %collective-permute-start = (bf16[312,1536]{1,0:T(8,128)(2,1)}, bf16[312,1536]{1,0:T(8,128)(2,1)S(1)}, u32[]{:S(2)}, u32[]{:S(2)}) collective-permute-start(bf16[312,1536]{1,0:T(8,128)(2,1)} %get-tuple-element.205), channel_id=1, source_target_pairs={{1,0},{2,1},{3,2},{4,3},{5,4},{6,5},{7,6},{8,7},{9,8},{10,9},{11,1... | collective-permute-start | bytes 2875400 | tf_op jit(solution)/shard_map/while/body/eval_jaxpr/ppermute | solution.py:10
  286.4 16.8 %collective-permute-start = (bf16[312,1536]{1,0:T(8,128)(2,1)}, bf16[312,1536]{1,0:T(8,128)(2,1)S(1)}, u32[]{:S(2)}, u32[]{:S(2)}) collective-permute-start(bf16[312,1536]{1,0:T(8,128)(2,1)} %get-tuple-element.205), channel_id=1, source_target_pairs={{1,0},{2,1},{3,2},{4,3},{5,4},{6,5},{7,6},{8,7},{9,8},{10,9},{11,1... | collective-permute-start | bytes 2875400 | tf_op jit(solution)/shard_map/while/body/eval_jaxpr/ppermute | solution.py:10
  305.7 16.8 %collective-permute-start = (bf16[312,1536]{1,0:T(8,128)(2,1)}, bf16[312,1536]{1,0:T(8,128)(2,1)S(1)}, u32[]{:S(2)}, u32[]{:S(2)}) collective-permute-start(bf16[312,1536]{1,0:T(8,128)(2,1)} %get-tuple-element.205), channel_id=1, source_target_pairs={{1,0},{2,1},{3,2},{4,3},{5,4},{6,5},{7,6},{8,7},{9,8},{10,9},{11,1... | collective-permute-start | bytes 2875400 | tf_op jit(solution)/shard_map/while/body/eval_jaxpr/ppermute | solution.py:10
  324.9 16.8 %collective-permute-start = (bf16[312,1536]{1,0:T(8,128)(2,1)}, bf16[312,1536]{1,0:T(8,128)(2,1)S(1)}, u32[]{:S(2)}, u32[]{:S(2)}) collective-permute-start(bf16[312,1536]{1,0:T(8,128)(2,1)} %get-tuple-element.205), channel_id=1, source_target_pairs={{1,0},{2,1},{3,2},{4,3},{5,4},{6,5},{7,6},{8,7},{9,8},{10,9},{11,1... | collective-permute-start | bytes 2875400 | tf_op jit(solution)/shard_map/while/body/eval_jaxpr/ppermute | solution.py:10
  344.1 16.8 %collective-permute-start = (bf16[312,1536]{1,0:T(8,128)(2,1)}, bf16[312,1536]{1,0:T(8,128)(2,1)S(1)}, u32[]{:S(2)}, u32[]{:S(2)}) collective-permute-start(bf16[312,1536]{1,0:T(8,128)(2,1)} %get-tuple-element.205), channel_id=1, source_target_pairs={{1,0},{2,1},{3,2},{4,3},{5,4},{6,5},{7,6},{8,7},{9,8},{10,9},{11,1... | collective-permute-start | bytes 2875400 | tf_op jit(solution)/shard_map/while/body/eval_jaxpr/ppermute | solution.py:10
  363.2 16.8 %collective-permute-start = (bf16[312,1536]{1,0:T(8,128)(2,1)}, bf16[312,1536]{1,0:T(8,128)(2,1)S(1)}, u32[]{:S(2)}, u32[]{:S(2)}) collective-permute-start(bf16[312,1536]{1,0:T(8,128)(2,1)} %get-tuple-element.205), channel_id=1, source_target_pairs={{1,0},{2,1},{3,2},{4,3},{5,4},{6,5},{7,6},{8,7},{9,8},{10,9},{11,1... | collective-permute-start | bytes 2875400 | tf_op jit(solution)/shard_map/while/body/eval_jaxpr/ppermute | solution.py:10
  382.5 16.8 %collective-permute-start = (bf16[312,1536]{1,0:T(8,128)(2,1)}, bf16[312,1536]{1,0:T(8,128)(2,1)S(1)}, u32[]{:S(2)}, u32[]{:S(2)}) collective-permute-start(bf16[312,1536]{1,0:T(8,128)(2,1)} %get-tuple-element.205), channel_id=1, source_target_pairs={{1,0},{2,1},{3,2},{4,3},{5,4},{6,5},{7,6},{8,7},{9,8},{10,9},{11,1... | collective-permute-start | bytes 2875400 | tf_op jit(solution)/shard_map/while/body/eval_jaxpr/ppermute | solution.py:10
  401.7 16.8 %collective-permute-start = (bf16[312,1536]{1,0:T(8,128)(2,1)}, bf16[312,1536]{1,0:T(8,128)(2,1)S(1)}, u32[]{:S(2)}, u32[]{:S(2)}) collective-permute-start(bf16[312,1536]{1,0:T(8,128)(2,1)} %get-tuple-element.205), channel_id=1, source_target_pairs={{1,0},{2,1},{3,2},{4,3},{5,4},{6,5},{7,6},{8,7},{9,8},{10,9},{11,1... | collective-permute-start | bytes 2875400 | tf_op jit(solution)/shard_map/while/body/eval_jaxpr/ppermute | solution.py:10
  420.9 16.8 %collective-permute-start = (bf16[312,1536]{1,0:T(8,128)(2,1)}, bf16[312,1536]{1,0:T(8,128)(2,1)S(1)}, u32[]{:S(2)}, u32[]{:S(2)}) collective-permute-start(bf16[312,1536]{1,0:T(8,128)(2,1)} %get-tuple-element.205), channel_id=1, source_target_pairs={{1,0},{2,1},{3,2},{4,3},{5,4},{6,5},{7,6},{8,7},{9,8},{10,9},{11,1... | collective-permute-start | bytes 2875400 | tf_op jit(solution)/shard_map/while/body/eval_jaxpr/ppermute | solution.py:10
  440.1 16.8 %collective-permute-start = (bf16[312,1536]{1,0:T(8,128)(2,1)}, bf16[312,1536]{1,0:T(8,128)(2,1)S(1)}, u32[]{:S(2)}, u32[]{:S(2)}) collective-permute-start(bf16[312,1536]{1,0:T(8,128)(2,1)} %get-tuple-element.205), channel_id=1, source_target_pairs={{1,0},{2,1},{3,2},{4,3},{5,4},{6,5},{7,6},{8,7},{9,8},{10,9},{11,1... | collective-permute-start | bytes 2875400 | tf_op jit(solution)/shard_map/while/body/eval_jaxpr/ppermute | solution.py:10
  459.3 16.8 %collective-permute-start = (bf16[312,1536]{1,0:T(8,128)(2,1)}, bf16[312,1536]{1,0:T(8,128)(2,1)S(1)}, u32[]{:S(2)}, u32[]{:S(2)}) collective-permute-start(bf16[312,1536]{1,0:T(8,128)(2,1)} %get-tuple-element.205), channel_id=1, source_target_pairs={{1,0},{2,1},{3,2},{4,3},{5,4},{6,5},{7,6},{8,7},{9,8},{10,9},{11,1... | collective-permute-start | bytes 2875400 | tf_op jit(solution)/shard_map/while/body/eval_jaxpr/ppermute | solution.py:10
  478.5 16.8 %collective-permute-start = (bf16[312,1536]{1,0:T(8,128)(2,1)}, bf16[312,1536]{1,0:T(8,128)(2,1)S(1)}, u32[]{:S(2)}, u32[]{:S(2)}) collective-permute-start(bf16[312,1536]{1,0:T(8,128)(2,1)} %get-tuple-element.205), channel_id=1, source_target_pairs={{1,0},{2,1},{3,2},{4,3},{5,4},{6,5},{7,6},{8,7},{9,8},{10,9},{11,1... | collective-permute-start | bytes 2875400 | tf_op jit(solution)/shard_map/while/body/eval_jaxpr/ppermute | solution.py:10
  497.7 16.8 %collective-permute-start = (bf16[312,1536]{1,0:T(8,128)(2,1)}, bf16[312,1536]{1,0:T(8,128)(2,1)S(1)}, u32[]{:S(2)}, u32[]{:S(2)}) collective-permute-start(bf16[312,1536]{1,0:T(8,128)(2,1)} %get-tuple-element.205), channel_id=1, source_target_pairs={{1,0},{2,1},{3,2},{4,3},{5,4},{6,5},{7,6},{8,7},{9,8},{10,9},{11,1... | collective-permute-start | bytes 2875400 | tf_op jit(solution)/shard_map/while/body/eval_jaxpr/ppermute | solution.py:10
  516.9 16.8 %collective-permute-start = (bf16[312,1536]{1,0:T(8,128)(2,1)}, bf16[312,1536]{1,0:T(8,128)(2,1)S(1)}, u32[]{:S(2)}, u32[]{:S(2)}) collective-permute-start(bf16[312,1536]{1,0:T(8,128)(2,1)} %get-tuple-element.205), channel_id=1, source_target_pairs={{1,0},{2,1},{3,2},{4,3},{5,4},{6,5},{7,6},{8,7},{9,8},{10,9},{11,1... | collective-permute-start | bytes 2875400 | tf_op jit(solution)/shard_map/while/body/eval_jaxpr/ppermute | solution.py:10
  536.1 16.8 %collective-permute-start = (bf16[312,1536]{1,0:T(8,128)(2,1)}, bf16[312,1536]{1,0:T(8,128)(2,1)S(1)}, u32[]{:S(2)}, u32[]{:S(2)}) collective-permute-start(bf16[312,1536]{1,0:T(8,128)(2,1)} %get-tuple-element.205), channel_id=1, source_target_pairs={{1,0},{2,1},{3,2},{4,3},{5,4},{6,5},{7,6},{8,7},{9,8},{10,9},{11,1... | collective-permute-start | bytes 2875400 | tf_op jit(solution)/shard_map/while/body/eval_jaxpr/ppermute | solution.py:10
  555.3 16.8 %collective-permute-start = (bf16[312,1536]{1,0:T(8,128)(2,1)}, bf16[312,1536]{1,0:T(8,128)(2,1)S(1)}, u32[]{:S(2)}, u32[]{:S(2)}) collective-permute-start(bf16[312,1536]{1,0:T(8,128)(2,1)} %get-tuple-element.205), channel_id=1, source_target_pairs={{1,0},{2,1},{3,2},{4,3},{5,4},{6,5},{7,6},{8,7},{9,8},{10,9},{11,1... | collective-permute-start | bytes 2875400 | tf_op jit(solution)/shard_map/while/body/eval_jaxpr/ppermute | solution.py:10
  574.6 16.7 %collective-permute-start = (bf16[312,1536]{1,0:T(8,128)(2,1)}, bf16[312,1536]{1,0:T(8,128)(2,1)S(1)}, u32[]{:S(2)}, u32[]{:S(2)}) collective-permute-start(bf16[312,1536]{1,0:T(8,128)(2,1)} %get-tuple-element.205), channel_id=1, source_target_pairs={{1,0},{2,1},{3,2},{4,3},{5,4},{6,5},{7,6},{8,7},{9,8},{10,9},{11,1... | collective-permute-start | bytes 2875400 | tf_op jit(solution)/shard_map/while/body/eval_jaxpr/ppermute | solution.py:10
  593.7 16.8 %collective-permute-start = (bf16[312,1536]{1,0:T(8,128)(2,1)}, bf16[312,1536]{1,0:T(8,128)(2,1)S(1)}, u32[]{:S(2)}, u32[]{:S(2)}) collective-permute-start(bf16[312,1536]{1,0:T(8,128)(2,1)} %get-tuple-element.205), channel_id=1, source_target_pairs={{1,0},{2,1},{3,2},{4,3},{5,4},{6,5},{7,6},{8,7},{9,8},{10,9},{11,1... | collective-permute-start | bytes 2875400 | tf_op jit(solution)/shard_map/while/body/eval_jaxpr/ppermute | solution.py:10
  612.9 16.7 %collective-permute-start = (bf16[312,1536]{1,0:T(8,128)(2,1)}, bf16[312,1536]{1,0:T(8,128)(2,1)S(1)}, u32[]{:S(2)}, u32[]{:S(2)}) collective-permute-start(bf16[312,1536]{1,0:T(8,128)(2,1)} %get-tuple-element.205), channel_id=1, source_target_pairs={{1,0},{2,1},{3,2},{4,3},{5,4},{6,5},{7,6},{8,7},{9,8},{10,9},{11,1... | collective-permute-start | bytes 2875400 | tf_op jit(solution)/shard_map/while/body/eval_jaxpr/ppermute | solution.py:10
  632.1 16.9 %collective-permute-start = (bf16[312,1536]{1,0:T(8,128)(2,1)}, bf16[312,1536]{1,0:T(8,128)(2,1)S(1)}, u32[]{:S(2)}, u32[]{:S(2)}) collective-permute-start(bf16[312,1536]{1,0:T(8,128)(2,1)} %get-tuple-element.205), channel_id=1, source_target_pairs={{1,0},{2,1},{3,2},{4,3},{5,4},{6,5},{7,6},{8,7},{9,8},{10,9},{11,1... | collective-permute-start | bytes 2875400 | tf_op jit(solution)/shard_map/while/body/eval_jaxpr/ppermute | solution.py:10
  651.3 16.8 %collective-permute-start = (bf16[312,1536]{1,0:T(8,128)(2,1)}, bf16[312,1536]{1,0:T(8,128)(2,1)S(1)}, u32[]{:S(2)}, u32[]{:S(2)}) collective-permute-start(bf16[312,1536]{1,0:T(8,128)(2,1)} %get-tuple-element.205), channel_id=1, source_target_pairs={{1,0},{2,1},{3,2},{4,3},{5,4},{6,5},{7,6},{8,7},{9,8},{10,9},{11,1... | collective-permute-start | bytes 2875400 | tf_op jit(solution)/shard_map/while/body/eval_jaxpr/ppermute | solution.py:10
  (2 other events, 18.9 us)
Sparse Core Ops, SparseCore 0:
  687.6 151.5 reduce-scatter.3
where the time goes:
time: 852 us; the launch traced here: 851 us
  starting transfers between devices  405 us (48%)
  waiting for transfers between devices  275 us (32%)
  local copies, waits for them, and re-layouts  109 us (13%)
  matrix products  46.3 us (5%)
  between operations  13.5 us (2%)
    ppermute x31, starting transfers between devices, shifted(): return lax.ppermute(block, axis, route)  396 us
    unnamed x2, waiting for transfers between devices  152 us
    ppermute x31, waiting for transfers between devices, shifted(): return lax.ppermute(block, axis, route)  108 us
    unnamed x7, local copies, waits for them, and re-layouts  51.1 us
    dot_general x32, matrix products, tile_with(): lax.dot_general(own_rows, visitor, (((1,), (1,)), ((), ())), preferred_el...  46.3 us
    while x31, local copies, waits for them, and re-layouts  29 us
    all_to_all x2, local copies, waits for them, and re-layouts, shards(): lax.all_to_all(masked, 'row', split_axis=0, concat_axis=2, tiled=True)  18.2 us
  transfers between devices with their start and end apart: 33, of which 33 were waited for; matrix products, arithmetic and copies ran while one was open for 0% of the time, Pallas kernels for 0%

commit v1 on v0

--- a/solution.py
+++ b/solution.py
@@ -18,7 +18,10 @@
     live_count = lax.dynamic_index_in_dim(aux_counts, group_index, 0, keepdims=False)
     live_mask = (jnp.arange(slot_count) < live_count).astype(jnp.bfloat16)
     masked = b_tensor * live_mask[None, :, None]
-    regrouped = lax.all_to_all(masked, "row", split_axis=0, concat_axis=2, tiled=True)
+    regrouped = jnp.concatenate(
+        lax.all_to_all(jnp.stack(jnp.split(masked, lax.axis_size("row"), axis=0)), "row", 0, 0),
+        axis=2,
+    )
     block_size = regrouped.shape[0]
     own_rows = regrouped.reshape(block_size, -1)
 

time: 852 us -> 793 us (0.931)
  local copies, waits for them, and re-layouts: 109 us -> 54.6 us
    while x31, local copies, waits for them, and re-layouts: 29 us -> 1.94 us
    all_to_all x2 -> x0, local copies, waits for them, and re-layouts: 18.2 us -> none  [shards(): lax.all_to_all(masked, 'row', split_axis=0, concat_axis=2, tiled=True)]
    unnamed x7 -> x36, local copies, waits for them, and re-layouts: 51.1 us -> 49 us
where the time goes in v1:
time: 793 us
  starting transfers between devices  404 us (51%)
  waiting for transfers between devices  272 us (34%)
  local copies, waits for them, and re-layouts  54.6 us (7%)
  matrix products  46.5 us (6%)
  between operations  13.5 us (2%)
    ppermute x31, starting transfers between devices, shifted(): return lax.ppermute(block, axis, route)  395 us
    unnamed x2, waiting for transfers between devices  152 us
    ppermute x31, waiting for transfers between devices, shifted(): return lax.ppermute(block, axis, route)  102 us
    unnamed x36, local copies, waits for them, and re-layouts  49 us
    dot_general x32, matrix products, tile_with(): lax.dot_general(own_rows, visitor, (((1,), (1,)), ((), ())), preferred_el...  46.5 us
    all_to_all x1, waiting for transfers between devices, shards(): lax.all_to_all(jnp.stack(jnp.split(masked, lax.axis_size('row'), axis=0))...  18.3 us
  transfers between devices with their start and end apart: 33, of which 33 were waited for; matrix products, arithmetic and copies ran while one was open for 0% of the time, Pallas kernels for 0%

profile of v1, /device:TPU:1, one launch (start us, length us, event | category | flops | bytes accessed | tf_op | source)
XLA Modules:
  0.0 792.7 jit_solution(7806280949627677660)
XLA Ops:
  41.4 18.3 %all-to-all-done = bf16[32,312,2,24]{1,3,2,0:T(8,128)(2,1)S(1)} async-done(((bf16[32,312,2,24]{1,3,2,0:T(8,128)(2,1)}), bf16[32,312,2,24]{1,3,2,0:T(8,128)(2,1)S(1)}, u32[]{:S(2)}, u32[]{:S(2)}) %all-to-all-start) | async-done | bytes 958496 | tf_op jit(solution)/shard_map/all_to_all | solution.py:22
  67.7 544.2 %while.17 = (s32[]{:T(128)}, bf16[312,1536]{1,0:T(8,128)(2,1)S(1)}, f32[312,32,312]{2,0,1:T(8,128)}, bf16[312,1536]{1,0:T(8,128)(2,1)S(1)}, s32[]{:T(128)}, /*index=5*/s32[]{:T(128)}, s32[]{:T(128)}, s32[]{:T(128)}, s32[]{:T(128)}) while((s32[]{:T(128)}, bf16[312,1536]{1,0:T(8,128)(2,1)S(1)}, f32[312,32,312]{2,0,1:T(8,128)}, ...), condition=%wide.region_1.2_spmd, body=%wide.region_0.1_spmd.sunk | while | flops 299040768 | bytes 8147236 | solution.py:43
  67.8 13.1 %collective-permute-done = bf16[312,1536]{1,0:T(8,128)(2,1)S(1)} collective-permute-done((bf16[312,1536]{1,0:T(8,128)(2,1)S(1)}, bf16[312,1536]{1,0:T(8,128)(2,1)S(1)}, u32[]{:S(2)}, u32[]{:S(2)}) %collective-permute-start) | collective-permute-done | bytes 958496 | tf_op jit(solution)/shard_map/while/body/eval_jaxpr/ppermute | solution.py:10
  82.6 13.1 %collective-permute-done = bf16[312,1536]{1,0:T(8,128)(2,1)S(1)} collective-permute-done((bf16[312,1536]{1,0:T(8,128)(2,1)S(1)}, bf16[312,1536]{1,0:T(8,128)(2,1)S(1)}, u32[]{:S(2)}, u32[]{:S(2)}) %collective-permute-start) | collective-permute-done | bytes 958496 | tf_op jit(solution)/shard_map/while/body/eval_jaxpr/ppermute | solution.py:10
  141.6 13.4 %collective-permute-start = (bf16[312,1536]{1,0:T(8,128)(2,1)S(1)}, bf16[312,1536]{1,0:T(8,128)(2,1)S(1)}, u32[]{:S(2)}, u32[]{:S(2)}) collective-permute-start(bf16[312,1536]{1,0:T(8,128)(2,1)S(1)} %get-tuple-element.350), channel_id=1, source_target_pairs={{1,0},{2,1},{3,2},{4,3},{5,4},{6,5},{7,6},{8,7},{9,8},{10,9},{11,1... | collective-permute-start | bytes 2875400 | tf_op jit(solution)/shard_map/while/body/eval_jaxpr/ppermute | solution.py:10
  158.8 14.5 %collective-permute-start = (bf16[312,1536]{1,0:T(8,128)(2,1)S(1)}, bf16[312,1536]{1,0:T(8,128)(2,1)S(1)}, u32[]{:S(2)}, u32[]{:S(2)}) collective-permute-start(bf16[312,1536]{1,0:T(8,128)(2,1)S(1)} %get-tuple-element.350), channel_id=1, source_target_pairs={{1,0},{2,1},{3,2},{4,3},{5,4},{6,5},{7,6},{8,7},{9,8},{10,9},{11,1... | collective-permute-start | bytes 2875400 | tf_op jit(solution)/shard_map/while/body/eval_jaxpr/ppermute | solution.py:10
  176.9 14.4 %collective-permute-start = (bf16[312,1536]{1,0:T(8,128)(2,1)S(1)}, bf16[312,1536]{1,0:T(8,128)(2,1)S(1)}, u32[]{:S(2)}, u32[]{:S(2)}) collective-permute-start(bf16[312,1536]{1,0:T(8,128)(2,1)S(1)} %get-tuple-element.350), channel_id=1, source_target_pairs={{1,0},{2,1},{3,2},{4,3},{5,4},{6,5},{7,6},{8,7},{9,8},{10,9},{11,1... | collective-permute-start | bytes 2875400 | tf_op jit(solution)/shard_map/while/body/eval_jaxpr/ppermute | solution.py:10
  195.0 14.4 %collective-permute-start = (bf16[312,1536]{1,0:T(8,128)(2,1)S(1)}, bf16[312,1536]{1,0:T(8,128)(2,1)S(1)}, u32[]{:S(2)}, u32[]{:S(2)}) collective-permute-start(bf16[312,1536]{1,0:T(8,128)(2,1)S(1)} %get-tuple-element.350), channel_id=1, source_target_pairs={{1,0},{2,1},{3,2},{4,3},{5,4},{6,5},{7,6},{8,7},{9,8},{10,9},{11,1... | collective-permute-start | bytes 2875400 | tf_op jit(solution)/shard_map/while/body/eval_jaxpr/ppermute | solution.py:10
  213.1 14.4 %collective-permute-start = (bf16[312,1536]{1,0:T(8,128)(2,1)S(1)}, bf16[312,1536]{1,0:T(8,128)(2,1)S(1)}, u32[]{:S(2)}, u32[]{:S(2)}) collective-permute-start(bf16[312,1536]{1,0:T(8,128)(2,1)S(1)} %get-tuple-element.350), channel_id=1, source_target_pairs={{1,0},{2,1},{3,2},{4,3},{5,4},{6,5},{7,6},{8,7},{9,8},{10,9},{11,1... | collective-permute-start | bytes 2875400 | tf_op jit(solution)/shard_map/while/body/eval_jaxpr/ppermute | solution.py:10
  231.3 14.4 %collective-permute-start = (bf16[312,1536]{1,0:T(8,128)(2,1)S(1)}, bf16[312,1536]{1,0:T(8,128)(2,1)S(1)}, u32[]{:S(2)}, u32[]{:S(2)}) collective-permute-start(bf16[312,1536]{1,0:T(8,128)(2,1)S(1)} %get-tuple-element.350), channel_id=1, source_target_pairs={{1,0},{2,1},{3,2},{4,3},{5,4},{6,5},{7,6},{8,7},{9,8},{10,9},{11,1... | collective-permute-start | bytes 2875400 | tf_op jit(solution)/shard_map/while/body/eval_jaxpr/ppermute | solution.py:10
  249.3 14.5 %collective-permute-start = (bf16[312,1536]{1,0:T(8,128)(2,1)S(1)}, bf16[312,1536]{1,0:T(8,128)(2,1)S(1)}, u32[]{:S(2)}, u32[]{:S(2)}) collective-permute-start(bf16[312,1536]{1,0:T(8,128)(2,1)S(1)} %get-tuple-element.350), channel_id=1, source_target_pairs={{1,0},{2,1},{3,2},{4,3},{5,4},{6,5},{7,6},{8,7},{9,8},{10,9},{11,1... | collective-permute-start | bytes 2875400 | tf_op jit(solution)/shard_map/while/body/eval_jaxpr/ppermute | solution.py:10
  267.5 14.4 %collective-permute-start = (bf16[312,1536]{1,0:T(8,128)(2,1)S(1)}, bf16[312,1536]{1,0:T(8,128)(2,1)S(1)}, u32[]{:S(2)}, u32[]{:S(2)}) collective-permute-start(bf16[312,1536]{1,0:T(8,128)(2,1)S(1)} %get-tuple-element.350), channel_id=1, source_target_pairs={{1,0},{2,1},{3,2},{4,3},{5,4},{6,5},{7,6},{8,7},{9,8},{10,9},{11,1... | collective-permute-start | bytes 2875400 | tf_op jit(solution)/shard_map/while/body/eval_jaxpr/ppermute | solution.py:10
  285.6 14.4 %collective-permute-start = (bf16[312,1536]{1,0:T(8,128)(2,1)S(1)}, bf16[312,1536]{1,0:T(8,128)(2,1)S(1)}, u32[]{:S(2)}, u32[]{:S(2)}) collective-permute-start(bf16[312,1536]{1,0:T(8,128)(2,1)S(1)} %get-tuple-element.350), channel_id=1, source_target_pairs={{1,0},{2,1},{3,2},{4,3},{5,4},{6,5},{7,6},{8,7},{9,8},{10,9},{11,1... | collective-permute-start | bytes 2875400 | tf_op jit(solution)/shard_map/while/body/eval_jaxpr/ppermute | solution.py:10
  303.7 14.4 %collective-permute-start = (bf16[312,1536]{1,0:T(8,128)(2,1)S(1)}, bf16[312,1536]{1,0:T(8,128)(2,1)S(1)}, u32[]{:S(2)}, u32[]{:S(2)}) collective-permute-start(bf16[312,1536]{1,0:T(8,128)(2,1)S(1)} %get-tuple-element.350), channel_id=1, source_target_pairs={{1,0},{2,1},{3,2},{4,3},{5,4},{6,5},{7,6},{8,7},{9,8},{10,9},{11,1... | collective-permute-start | bytes 2875400 | tf_op jit(solution)/shard_map/while/body/eval_jaxpr/ppermute | solution.py:10
  321.8 14.4 %collective-permute-start = (bf16[312,1536]{1,0:T(8,128)(2,1)S(1)}, bf16[312,1536]{1,0:T(8,128)(2,1)S(1)}, u32[]{:S(2)}, u32[]{:S(2)}) collective-permute-start(bf16[312,1536]{1,0:T(8,128)(2,1)S(1)} %get-tuple-element.350), channel_id=1, source_target_pairs={{1,0},{2,1},{3,2},{4,3},{5,4},{6,5},{7,6},{8,7},{9,8},{10,9},{11,1... | collective-permute-start | bytes 2875400 | tf_op jit(solution)/shard_map/while/body/eval_jaxpr/ppermute | solution.py:10
  340.0 14.4 %collective-permute-start = (bf16[312,1536]{1,0:T(8,128)(2,1)S(1)}, bf16[312,1536]{1,0:T(8,128)(2,1)S(1)}, u32[]{:S(2)}, u32[]{:S(2)}) collective-permute-start(bf16[312,1536]{1,0:T(8,128)(2,1)S(1)} %get-tuple-element.350), channel_id=1, source_target_pairs={{1,0},{2,1},{3,2},{4,3},{5,4},{6,5},{7,6},{8,7},{9,8},{10,9},{11,1... | collective-permute-start | bytes 2875400 | tf_op jit(solution)/shard_map/while/body/eval_jaxpr/ppermute | solution.py:10
  358.1 14.4 %collective-permute-start = (bf16[312,1536]{1,0:T(8,128)(2,1)S(1)}, bf16[312,1536]{1,0:T(8,128)(2,1)S(1)}, u32[]{:S(2)}, u32[]{:S(2)}) collective-permute-start(bf16[312,1536]{1,0:T(8,128)(2,1)S(1)} %get-tuple-element.350), channel_id=1, source_target_pairs={{1,0},{2,1},{3,2},{4,3},{5,4},{6,5},{7,6},{8,7},{9,8},{10,9},{11,1... | collective-permute-start | bytes 2875400 | tf_op jit(solution)/shard_map/while/body/eval_jaxpr/ppermute | solution.py:10
  376.3 14.4 %collective-permute-start = (bf16[312,1536]{1,0:T(8,128)(2,1)S(1)}, bf16[312,1536]{1,0:T(8,128)(2,1)S(1)}, u32[]{:S(2)}, u32[]{:S(2)}) collective-permute-start(bf16[312,1536]{1,0:T(8,128)(2,1)S(1)} %get-tuple-element.350), channel_id=1, source_target_pairs={{1,0},{2,1},{3,2},{4,3},{5,4},{6,5},{7,6},{8,7},{9,8},{10,9},{11,1... | collective-permute-start | bytes 2875400 | tf_op jit(solution)/shard_map/while/body/eval_jaxpr/ppermute | solution.py:10
  394.4 14.4 %collective-permute-start = (bf16[312,1536]{1,0:T(8,128)(2,1)S(1)}, bf16[312,1536]{1,0:T(8,128)(2,1)S(1)}, u32[]{:S(2)}, u32[]{:S(2)}) collective-permute-start(bf16[312,1536]{1,0:T(8,128)(2,1)S(1)} %get-tuple-element.350), channel_id=1, source_target_pairs={{1,0},{2,1},{3,2},{4,3},{5,4},{6,5},{7,6},{8,7},{9,8},{10,9},{11,1... | collective-permute-start | bytes 2875400 | tf_op jit(solution)/shard_map/while/body/eval_jaxpr/ppermute | solution.py:10
  412.5 14.5 %collective-permute-start = (bf16[312,1536]{1,0:T(8,128)(2,1)S(1)}, bf16[312,1536]{1,0:T(8,128)(2,1)S(1)}, u32[]{:S(2)}, u32[]{:S(2)}) collective-permute-start(bf16[312,1536]{1,0:T(8,128)(2,1)S(1)} %get-tuple-element.350), channel_id=1, source_target_pairs={{1,0},{2,1},{3,2},{4,3},{5,4},{6,5},{7,6},{8,7},{9,8},{10,9},{11,1... | collective-permute-start | bytes 2875400 | tf_op jit(solution)/shard_map/while/body/eval_jaxpr/ppermute | solution.py:10
  430.7 14.4 %collective-permute-start = (bf16[312,1536]{1,0:T(8,128)(2,1)S(1)}, bf16[312,1536]{1,0:T(8,128)(2,1)S(1)}, u32[]{:S(2)}, u32[]{:S(2)}) collective-permute-start(bf16[312,1536]{1,0:T(8,128)(2,1)S(1)} %get-tuple-element.350), channel_id=1, source_target_pairs={{1,0},{2,1},{3,2},{4,3},{5,4},{6,5},{7,6},{8,7},{9,8},{10,9},{11,1... | collective-permute-start | bytes 2875400 | tf_op jit(solution)/shard_map/while/body/eval_jaxpr/ppermute | solution.py:10
  448.8 14.5 %collective-permute-start = (bf16[312,1536]{1,0:T(8,128)(2,1)S(1)}, bf16[312,1536]{1,0:T(8,128)(2,1)S(1)}, u32[]{:S(2)}, u32[]{:S(2)}) collective-permute-start(bf16[312,1536]{1,0:T(8,128)(2,1)S(1)} %get-tuple-element.350), channel_id=1, source_target_pairs={{1,0},{2,1},{3,2},{4,3},{5,4},{6,5},{7,6},{8,7},{9,8},{10,9},{11,1... | collective-permute-start | bytes 2875400 | tf_op jit(solution)/shard_map/while/body/eval_jaxpr/ppermute | solution.py:10
  466.9 14.4 %collective-permute-start = (bf16[312,1536]{1,0:T(8,128)(2,1)S(1)}, bf16[312,1536]{1,0:T(8,128)(2,1)S(1)}, u32[]{:S(2)}, u32[]{:S(2)}) collective-permute-start(bf16[312,1536]{1,0:T(8,128)(2,1)S(1)} %get-tuple-element.350), channel_id=1, source_target_pairs={{1,0},{2,1},{3,2},{4,3},{5,4},{6,5},{7,6},{8,7},{9,8},{10,9},{11,1... | collective-permute-start | bytes 2875400 | tf_op jit(solution)/shard_map/while/body/eval_jaxpr/ppermute | solution.py:10
  485.0 14.4 %collective-permute-start = (bf16[312,1536]{1,0:T(8,128)(2,1)S(1)}, bf16[312,1536]{1,0:T(8,128)(2,1)S(1)}, u32[]{:S(2)}, u32[]{:S(2)}) collective-permute-start(bf16[312,1536]{1,0:T(8,128)(2,1)S(1)} %get-tuple-element.350), channel_id=1, source_target_pairs={{1,0},{2,1},{3,2},{4,3},{5,4},{6,5},{7,6},{8,7},{9,8},{10,9},{11,1... | collective-permute-start | bytes 2875400 | tf_op jit(solution)/shard_map/while/body/eval_jaxpr/ppermute | solution.py:10
  503.1 14.4 %collective-permute-start = (bf16[312,1536]{1,0:T(8,128)(2,1)S(1)}, bf16[312,1536]{1,0:T(8,128)(2,1)S(1)}, u32[]{:S(2)}, u32[]{:S(2)}) collective-permute-start(bf16[312,1536]{1,0:T(8,128)(2,1)S(1)} %get-tuple-element.350), channel_id=1, source_target_pairs={{1,0},{2,1},{3,2},{4,3},{5,4},{6,5},{7,6},{8,7},{9,8},{10,9},{11,1... | collective-permute-start | bytes 2875400 | tf_op jit(solution)/shard_map/while/body/eval_jaxpr/ppermute | solution.py:10
  521.3 14.4 %collective-permute-start = (bf16[312,1536]{1,0:T(8,128)(2,1)S(1)}, bf16[312,1536]{1,0:T(8,128)(2,1)S(1)}, u32[]{:S(2)}, u32[]{:S(2)}) collective-permute-start(bf16[312,1536]{1,0:T(8,128)(2,1)S(1)} %get-tuple-element.350), channel_id=1, source_target_pairs={{1,0},{2,1},{3,2},{4,3},{5,4},{6,5},{7,6},{8,7},{9,8},{10,9},{11,1... | collective-permute-start | bytes 2875400 | tf_op jit(solution)/shard_map/while/body/eval_jaxpr/ppermute | solution.py:10
  539.4 14.5 %collective-permute-start = (bf16[312,1536]{1,0:T(8,128)(2,1)S(1)}, bf16[312,1536]{1,0:T(8,128)(2,1)S(1)}, u32[]{:S(2)}, u32[]{:S(2)}) collective-permute-start(bf16[312,1536]{1,0:T(8,128)(2,1)S(1)} %get-tuple-element.350), channel_id=1, source_target_pairs={{1,0},{2,1},{3,2},{4,3},{5,4},{6,5},{7,6},{8,7},{9,8},{10,9},{11,1... | collective-permute-start | bytes 2875400 | tf_op jit(solution)/shard_map/while/body/eval_jaxpr/ppermute | solution.py:10
  557.6 14.4 %collective-permute-start = (bf16[312,1536]{1,0:T(8,128)(2,1)S(1)}, bf16[312,1536]{1,0:T(8,128)(2,1)S(1)}, u32[]{:S(2)}, u32[]{:S(2)}) collective-permute-start(bf16[312,1536]{1,0:T(8,128)(2,1)S(1)} %get-tuple-element.350), channel_id=1, source_target_pairs={{1,0},{2,1},{3,2},{4,3},{5,4},{6,5},{7,6},{8,7},{9,8},{10,9},{11,1... | collective-permute-start | bytes 2875400 | tf_op jit(solution)/shard_map/while/body/eval_jaxpr/ppermute | solution.py:10
  575.6 14.5 %collective-permute-start = (bf16[312,1536]{1,0:T(8,128)(2,1)S(1)}, bf16[312,1536]{1,0:T(8,128)(2,1)S(1)}, u32[]{:S(2)}, u32[]{:S(2)}) collective-permute-start(bf16[312,1536]{1,0:T(8,128)(2,1)S(1)} %get-tuple-element.350), channel_id=1, source_target_pairs={{1,0},{2,1},{3,2},{4,3},{5,4},{6,5},{7,6},{8,7},{9,8},{10,9},{11,1... | collective-permute-start | bytes 2875400 | tf_op jit(solution)/shard_map/while/body/eval_jaxpr/ppermute | solution.py:10
  593.8 14.4 %collective-permute-start = (bf16[312,1536]{1,0:T(8,128)(2,1)S(1)}, bf16[312,1536]{1,0:T(8,128)(2,1)S(1)}, u32[]{:S(2)}, u32[]{:S(2)}) collective-permute-start(bf16[312,1536]{1,0:T(8,128)(2,1)S(1)} %get-tuple-element.350), channel_id=1, source_target_pairs={{1,0},{2,1},{3,2},{4,3},{5,4},{6,5},{7,6},{8,7},{9,8},{10,9},{11,1... | collective-permute-start | bytes 2875400 | tf_op jit(solution)/shard_map/while/body/eval_jaxpr/ppermute | solution.py:10
  611.9 16.9 %copy.1130 = f32[312,32,312]{0,2,1:T(8,128)} copy(f32[312,32,312]{2,0,1:T(8,128)} %get-tuple-element.138) | data formatting | bytes 24920064
  628.9 151.8 %reduce-scatter.4.cloned.1.call-done = f32[2496,312]{1,0:T(8,128)} async-done(((f32[9984,312]{1,0:T(8,128)}), f32[2496,312]{1,0:T(8,128)}) %reduce-scatter.4.cloned.1.call-update) | async-done | bytes 3115024
  (142 shorter events, 191.7 us)
Async XLA Ops:
  32.0 27.8 %all-to-all-start = ((bf16[32,312,2,24]{1,3,2,0:T(8,128)(2,1)}), bf16[32,312,2,24]{1,3,2,0:T(8,128)(2,1)S(1)}, u32[]{:S(2)}, u32[]{:S(2)}) async-start(bf16[32,312,2,24]{1,3,2,0:T(8,128)(2,1)} %constant_dynamic-update-slice_fusion), calls=%async_computation | async-start | bytes 2359296 | tf_op jit(solution)/shard_map/all_to_all | solution.py:22
  41.4 739.3 %reduce-scatter.4.cloned.1.call-start = ((), (), s32[]{:S(2)}) async-start(), calls=%async_computation.2 | async-start | bytes 19169280
  67.7 13.3 %collective-permute-start = (bf16[312,1536]{1,0:T(8,128)(2,1)S(1)}, bf16[312,1536]{1,0:T(8,128)(2,1)S(1)}, u32[]{:S(2)}, u32[]{:S(2)}) collective-permute-start(bf16[312,1536]{1,0:T(8,128)(2,1)S(1)} %get-tuple-element.350), channel_id=1, source_target_pairs={{1,0},{2,1},{3,2},{4,3},{5,4},{6,5},{7,6},{8,7},{9,8},{10,9},{11,1... | collective-permute-start | bytes 2875400 | tf_op jit(solution)/shard_map/while/body/eval_jaxpr/ppermute | solution.py:10
  82.5 13.3 %collective-permute-start = (bf16[312,1536]{1,0:T(8,128)(2,1)S(1)}, bf16[312,1536]{1,0:T(8,128)(2,1)S(1)}, u32[]{:S(2)}, u32[]{:S(2)}) collective-permute-start(bf16[312,1536]{1,0:T(8,128)(2,1)S(1)} %get-tuple-element.350), channel_id=1, source_target_pairs={{1,0},{2,1},{3,2},{4,3},{5,4},{6,5},{7,6},{8,7},{9,8},{10,9},{11,1... | collective-permute-start | bytes 2875400 | tf_op jit(solution)/shard_map/while/body/eval_jaxpr/ppermute | solution.py:10
  97.3 13.3 %collective-permute-start = (bf16[312,1536]{1,0:T(8,128)(2,1)S(1)}, bf16[312,1536]{1,0:T(8,128)(2,1)S(1)}, u32[]{:S(2)}, u32[]{:S(2)}) collective-permute-start(bf16[312,1536]{1,0:T(8,128)(2,1)S(1)} %get-tuple-element.350), channel_id=1, source_target_pairs={{1,0},{2,1},{3,2},{4,3},{5,4},{6,5},{7,6},{8,7},{9,8},{10,9},{11,1... | collective-permute-start | bytes 2875400 | tf_op jit(solution)/shard_map/while/body/eval_jaxpr/ppermute | solution.py:10
  112.1 13.3 %collective-permute-start = (bf16[312,1536]{1,0:T(8,128)(2,1)S(1)}, bf16[312,1536]{1,0:T(8,128)(2,1)S(1)}, u32[]{:S(2)}, u32[]{:S(2)}) collective-permute-start(bf16[312,1536]{1,0:T(8,128)(2,1)S(1)} %get-tuple-element.350), channel_id=1, source_target_pairs={{1,0},{2,1},{3,2},{4,3},{5,4},{6,5},{7,6},{8,7},{9,8},{10,9},{11,1... | collective-permute-start | bytes 2875400 | tf_op jit(solution)/shard_map/while/body/eval_jaxpr/ppermute | solution.py:10
  141.6 15.6 %collective-permute-start = (bf16[312,1536]{1,0:T(8,128)(2,1)S(1)}, bf16[312,1536]{1,0:T(8,128)(2,1)S(1)}, u32[]{:S(2)}, u32[]{:S(2)}) collective-permute-start(bf16[312,1536]{1,0:T(8,128)(2,1)S(1)} %get-tuple-element.350), channel_id=1, source_target_pairs={{1,0},{2,1},{3,2},{4,3},{5,4},{6,5},{7,6},{8,7},{9,8},{10,9},{11,1... | collective-permute-start | bytes 2875400 | tf_op jit(solution)/shard_map/while/body/eval_jaxpr/ppermute | solution.py:10
  158.8 16.6 %collective-permute-start = (bf16[312,1536]{1,0:T(8,128)(2,1)S(1)}, bf16[312,1536]{1,0:T(8,128)(2,1)S(1)}, u32[]{:S(2)}, u32[]{:S(2)}) collective-permute-start(bf16[312,1536]{1,0:T(8,128)(2,1)S(1)} %get-tuple-element.350), channel_id=1, source_target_pairs={{1,0},{2,1},{3,2},{4,3},{5,4},{6,5},{7,6},{8,7},{9,8},{10,9},{11,1... | collective-permute-start | bytes 2875400 | tf_op jit(solution)/shard_map/while/body/eval_jaxpr/ppermute | solution.py:10
  176.9 16.6 %collective-permute-start = (bf16[312,1536]{1,0:T(8,128)(2,1)S(1)}, bf16[312,1536]{1,0:T(8,128)(2,1)S(1)}, u32[]{:S(2)}, u32[]{:S(2)}) collective-permute-start(bf16[312,1536]{1,0:T(8,128)(2,1)S(1)} %get-tuple-element.350), channel_id=1, source_target_pairs={{1,0},{2,1},{3,2},{4,3},{5,4},{6,5},{7,6},{8,7},{9,8},{10,9},{11,1... | collective-permute-start | bytes 2875400 | tf_op jit(solution)/shard_map/while/body/eval_jaxpr/ppermute | solution.py:10
  195.0 16.6 %collective-permute-start = (bf16[312,1536]{1,0:T(8,128)(2,1)S(1)}, bf16[312,1536]{1,0:T(8,128)(2,1)S(1)}, u32[]{:S(2)}, u32[]{:S(2)}) collective-permute-start(bf16[312,1536]{1,0:T(8,128)(2,1)S(1)} %get-tuple-element.350), channel_id=1, source_target_pairs={{1,0},{2,1},{3,2},{4,3},{5,4},{6,5},{7,6},{8,7},{9,8},{10,9},{11,1... | collective-permute-start | bytes 2875400 | tf_op jit(solution)/shard_map/while/body/eval_jaxpr/ppermute | solution.py:10
  213.1 16.6 %collective-permute-start = (bf16[312,1536]{1,0:T(8,128)(2,1)S(1)}, bf16[312,1536]{1,0:T(8,128)(2,1)S(1)}, u32[]{:S(2)}, u32[]{:S(2)}) collective-permute-start(bf16[312,1536]{1,0:T(8,128)(2,1)S(1)} %get-tuple-element.350), channel_id=1, source_target_pairs={{1,0},{2,1},{3,2},{4,3},{5,4},{6,5},{7,6},{8,7},{9,8},{10,9},{11,1... | collective-permute-start | bytes 2875400 | tf_op jit(solution)/shard_map/while/body/eval_jaxpr/ppermute | solution.py:10
  231.3 16.5 %collective-permute-start = (bf16[312,1536]{1,0:T(8,128)(2,1)S(1)}, bf16[312,1536]{1,0:T(8,128)(2,1)S(1)}, u32[]{:S(2)}, u32[]{:S(2)}) collective-permute-start(bf16[312,1536]{1,0:T(8,128)(2,1)S(1)} %get-tuple-element.350), channel_id=1, source_target_pairs={{1,0},{2,1},{3,2},{4,3},{5,4},{6,5},{7,6},{8,7},{9,8},{10,9},{11,1... | collective-permute-start | bytes 2875400 | tf_op jit(solution)/shard_map/while/body/eval_jaxpr/ppermute | solution.py:10
  249.3 16.6 %collective-permute-start = (bf16[312,1536]{1,0:T(8,128)(2,1)S(1)}, bf16[312,1536]{1,0:T(8,128)(2,1)S(1)}, u32[]{:S(2)}, u32[]{:S(2)}) collective-permute-start(bf16[312,1536]{1,0:T(8,128)(2,1)S(1)} %get-tuple-element.350), channel_id=1, source_target_pairs={{1,0},{2,1},{3,2},{4,3},{5,4},{6,5},{7,6},{8,7},{9,8},{10,9},{11,1... | collective-permute-start | bytes 2875400 | tf_op jit(solution)/shard_map/while/body/eval_jaxpr/ppermute | solution.py:10
  267.5 16.5 %collective-permute-start = (bf16[312,1536]{1,0:T(8,128)(2,1)S(1)}, bf16[312,1536]{1,0:T(8,128)(2,1)S(1)}, u32[]{:S(2)}, u32[]{:S(2)}) collective-permute-start(bf16[312,1536]{1,0:T(8,128)(2,1)S(1)} %get-tuple-element.350), channel_id=1, source_target_pairs={{1,0},{2,1},{3,2},{4,3},{5,4},{6,5},{7,6},{8,7},{9,8},{10,9},{11,1... | collective-permute-start | bytes 2875400 | tf_op jit(solution)/shard_map/while/body/eval_jaxpr/ppermute | solution.py:10
  285.6 16.6 %collective-permute-start = (bf16[312,1536]{1,0:T(8,128)(2,1)S(1)}, bf16[312,1536]{1,0:T(8,128)(2,1)S(1)}, u32[]{:S(2)}, u32[]{:S(2)}) collective-permute-start(bf16[312,1536]{1,0:T(8,128)(2,1)S(1)} %get-tuple-element.350), channel_id=1, source_target_pairs={{1,0},{2,1},{3,2},{4,3},{5,4},{6,5},{7,6},{8,7},{9,8},{10,9},{11,1... | collective-permute-start | bytes 2875400 | tf_op jit(solution)/shard_map/while/body/eval_jaxpr/ppermute | solution.py:10
  303.7 16.6 %collective-permute-start = (bf16[312,1536]{1,0:T(8,128)(2,1)S(1)}, bf16[312,1536]{1,0:T(8,128)(2,1)S(1)}, u32[]{:S(2)}, u32[]{:S(2)}) collective-permute-start(bf16[312,1536]{1,0:T(8,128)(2,1)S(1)} %get-tuple-element.350), channel_id=1, source_target_pairs={{1,0},{2,1},{3,2},{4,3},{5,4},{6,5},{7,6},{8,7},{9,8},{10,9},{11,1... | collective-permute-start | bytes 2875400 | tf_op jit(solution)/shard_map/while/body/eval_jaxpr/ppermute | solution.py:10
  321.8 16.6 %collective-permute-start = (bf16[312,1536]{1,0:T(8,128)(2,1)S(1)}, bf16[312,1536]{1,0:T(8,128)(2,1)S(1)}, u32[]{:S(2)}, u32[]{:S(2)}) collective-permute-start(bf16[312,1536]{1,0:T(8,128)(2,1)S(1)} %get-tuple-element.350), channel_id=1, source_target_pairs={{1,0},{2,1},{3,2},{4,3},{5,4},{6,5},{7,6},{8,7},{9,8},{10,9},{11,1... | collective-permute-start | bytes 2875400 | tf_op jit(solution)/shard_map/while/body/eval_jaxpr/ppermute | solution.py:10
  340.0 16.5 %collective-permute-start = (bf16[312,1536]{1,0:T(8,128)(2,1)S(1)}, bf16[312,1536]{1,0:T(8,128)(2,1)S(1)}, u32[]{:S(2)}, u32[]{:S(2)}) collective-permute-start(bf16[312,1536]{1,0:T(8,128)(2,1)S(1)} %get-tuple-element.350), channel_id=1, source_target_pairs={{1,0},{2,1},{3,2},{4,3},{5,4},{6,5},{7,6},{8,7},{9,8},{10,9},{11,1... | collective-permute-start | bytes 2875400 | tf_op jit(solution)/shard_map/while/body/eval_jaxpr/ppermute | solution.py:10
  358.1 16.6 %collective-permute-start = (bf16[312,1536]{1,0:T(8,128)(2,1)S(1)}, bf16[312,1536]{1,0:T(8,128)(2,1)S(1)}, u32[]{:S(2)}, u32[]{:S(2)}) collective-permute-start(bf16[312,1536]{1,0:T(8,128)(2,1)S(1)} %get-tuple-element.350), channel_id=1, source_target_pairs={{1,0},{2,1},{3,2},{4,3},{5,4},{6,5},{7,6},{8,7},{9,8},{10,9},{11,1... | collective-permute-start | bytes 2875400 | tf_op jit(solution)/shard_map/while/body/eval_jaxpr/ppermute | solution.py:10
  376.3 16.5 %collective-permute-start = (bf16[312,1536]{1,0:T(8,128)(2,1)S(1)}, bf16[312,1536]{1,0:T(8,128)(2,1)S(1)}, u32[]{:S(2)}, u32[]{:S(2)}) collective-permute-start(bf16[312,1536]{1,0:T(8,128)(2,1)S(1)} %get-tuple-element.350), channel_id=1, source_target_pairs={{1,0},{2,1},{3,2},{4,3},{5,4},{6,5},{7,6},{8,7},{9,8},{10,9},{11,1... | collective-permute-start | bytes 2875400 | tf_op jit(solution)/shard_map/while/body/eval_jaxpr/ppermute | solution.py:10
  394.4 16.6 %collective-permute-start = (bf16[312,1536]{1,0:T(8,128)(2,1)S(1)}, bf16[312,1536]{1,0:T(8,128)(2,1)S(1)}, u32[]{:S(2)}, u32[]{:S(2)}) collective-permute-start(bf16[312,1536]{1,0:T(8,128)(2,1)S(1)} %get-tuple-element.350), channel_id=1, source_target_pairs={{1,0},{2,1},{3,2},{4,3},{5,4},{6,5},{7,6},{8,7},{9,8},{10,9},{11,1... | collective-permute-start | bytes 2875400 | tf_op jit(solution)/shard_map/while/body/eval_jaxpr/ppermute | solution.py:10
  412.5 16.6 %collective-permute-start = (bf16[312,1536]{1,0:T(8,128)(2,1)S(1)}, bf16[312,1536]{1,0:T(8,128)(2,1)S(1)}, u32[]{:S(2)}, u32[]{:S(2)}) collective-permute-start(bf16[312,1536]{1,0:T(8,128)(2,1)S(1)} %get-tuple-element.350), channel_id=1, source_target_pairs={{1,0},{2,1},{3,2},{4,3},{5,4},{6,5},{7,6},{8,7},{9,8},{10,9},{11,1... | collective-permute-start | bytes 2875400 | tf_op jit(solution)/shard_map/while/body/eval_jaxpr/ppermute | solution.py:10
  430.7 16.6 %collective-permute-start = (bf16[312,1536]{1,0:T(8,128)(2,1)S(1)}, bf16[312,1536]{1,0:T(8,128)(2,1)S(1)}, u32[]{:S(2)}, u32[]{:S(2)}) collective-permute-start(bf16[312,1536]{1,0:T(8,128)(2,1)S(1)} %get-tuple-element.350), channel_id=1, source_target_pairs={{1,0},{2,1},{3,2},{4,3},{5,4},{6,5},{7,6},{8,7},{9,8},{10,9},{11,1... | collective-permute-start | bytes 2875400 | tf_op jit(solution)/shard_map/while/body/eval_jaxpr/ppermute | solution.py:10
  448.8 16.6 %collective-permute-start = (bf16[312,1536]{1,0:T(8,128)(2,1)S(1)}, bf16[312,1536]{1,0:T(8,128)(2,1)S(1)}, u32[]{:S(2)}, u32[]{:S(2)}) collective-permute-start(bf16[312,1536]{1,0:T(8,128)(2,1)S(1)} %get-tuple-element.350), channel_id=1, source_target_pairs={{1,0},{2,1},{3,2},{4,3},{5,4},{6,5},{7,6},{8,7},{9,8},{10,9},{11,1... | collective-permute-start | bytes 2875400 | tf_op jit(solution)/shard_map/while/body/eval_jaxpr/ppermute | solution.py:10
  466.9 16.6 %collective-permute-start = (bf16[312,1536]{1,0:T(8,128)(2,1)S(1)}, bf16[312,1536]{1,0:T(8,128)(2,1)S(1)}, u32[]{:S(2)}, u32[]{:S(2)}) collective-permute-start(bf16[312,1536]{1,0:T(8,128)(2,1)S(1)} %get-tuple-element.350), channel_id=1, source_target_pairs={{1,0},{2,1},{3,2},{4,3},{5,4},{6,5},{7,6},{8,7},{9,8},{10,9},{11,1... | collective-permute-start | bytes 2875400 | tf_op jit(solution)/shard_map/while/body/eval_jaxpr/ppermute | solution.py:10
  485.0 16.6 %collective-permute-start = (bf16[312,1536]{1,0:T(8,128)(2,1)S(1)}, bf16[312,1536]{1,0:T(8,128)(2,1)S(1)}, u32[]{:S(2)}, u32[]{:S(2)}) collective-permute-start(bf16[312,1536]{1,0:T(8,128)(2,1)S(1)} %get-tuple-element.350), channel_id=1, source_target_pairs={{1,0},{2,1},{3,2},{4,3},{5,4},{6,5},{7,6},{8,7},{9,8},{10,9},{11,1... | collective-permute-start | bytes 2875400 | tf_op jit(solution)/shard_map/while/body/eval_jaxpr/ppermute | solution.py:10
  503.1 16.6 %collective-permute-start = (bf16[312,1536]{1,0:T(8,128)(2,1)S(1)}, bf16[312,1536]{1,0:T(8,128)(2,1)S(1)}, u32[]{:S(2)}, u32[]{:S(2)}) collective-permute-start(bf16[312,1536]{1,0:T(8,128)(2,1)S(1)} %get-tuple-element.350), channel_id=1, source_target_pairs={{1,0},{2,1},{3,2},{4,3},{5,4},{6,5},{7,6},{8,7},{9,8},{10,9},{11,1... | collective-permute-start | bytes 2875400 | tf_op jit(solution)/shard_map/while/body/eval_jaxpr/ppermute | solution.py:10
  521.3 16.5 %collective-permute-start = (bf16[312,1536]{1,0:T(8,128)(2,1)S(1)}, bf16[312,1536]{1,0:T(8,128)(2,1)S(1)}, u32[]{:S(2)}, u32[]{:S(2)}) collective-permute-start(bf16[312,1536]{1,0:T(8,128)(2,1)S(1)} %get-tuple-element.350), channel_id=1, source_target_pairs={{1,0},{2,1},{3,2},{4,3},{5,4},{6,5},{7,6},{8,7},{9,8},{10,9},{11,1... | collective-permute-start | bytes 2875400 | tf_op jit(solution)/shard_map/while/body/eval_jaxpr/ppermute | solution.py:10
  539.4 16.6 %collective-permute-start = (bf16[312,1536]{1,0:T(8,128)(2,1)S(1)}, bf16[312,1536]{1,0:T(8,128)(2,1)S(1)}, u32[]{:S(2)}, u32[]{:S(2)}) collective-permute-start(bf16[312,1536]{1,0:T(8,128)(2,1)S(1)} %get-tuple-element.350), channel_id=1, source_target_pairs={{1,0},{2,1},{3,2},{4,3},{5,4},{6,5},{7,6},{8,7},{9,8},{10,9},{11,1... | collective-permute-start | bytes 2875400 | tf_op jit(solution)/shard_map/while/body/eval_jaxpr/ppermute | solution.py:10
  557.6 16.5 %collective-permute-start = (bf16[312,1536]{1,0:T(8,128)(2,1)S(1)}, bf16[312,1536]{1,0:T(8,128)(2,1)S(1)}, u32[]{:S(2)}, u32[]{:S(2)}) collective-permute-start(bf16[312,1536]{1,0:T(8,128)(2,1)S(1)} %get-tuple-element.350), channel_id=1, source_target_pairs={{1,0},{2,1},{3,2},{4,3},{5,4},{6,5},{7,6},{8,7},{9,8},{10,9},{11,1... | collective-permute-start | bytes 2875400 | tf_op jit(solution)/shard_map/while/body/eval_jaxpr/ppermute | solution.py:10
  575.6 16.7 %collective-permute-start = (bf16[312,1536]{1,0:T(8,128)(2,1)S(1)}, bf16[312,1536]{1,0:T(8,128)(2,1)S(1)}, u32[]{:S(2)}, u32[]{:S(2)}) collective-permute-start(bf16[312,1536]{1,0:T(8,128)(2,1)S(1)} %get-tuple-element.350), channel_id=1, source_target_pairs={{1,0},{2,1},{3,2},{4,3},{5,4},{6,5},{7,6},{8,7},{9,8},{10,9},{11,1... | collective-permute-start | bytes 2875400 | tf_op jit(solution)/shard_map/while/body/eval_jaxpr/ppermute | solution.py:10
  593.8 16.6 %collective-permute-start = (bf16[312,1536]{1,0:T(8,128)(2,1)S(1)}, bf16[312,1536]{1,0:T(8,128)(2,1)S(1)}, u32[]{:S(2)}, u32[]{:S(2)}) collective-permute-start(bf16[312,1536]{1,0:T(8,128)(2,1)S(1)} %get-tuple-element.350), channel_id=1, source_target_pairs={{1,0},{2,1},{3,2},{4,3},{5,4},{6,5},{7,6},{8,7},{9,8},{10,9},{11,1... | collective-permute-start | bytes 2875400 | tf_op jit(solution)/shard_map/while/body/eval_jaxpr/ppermute | solution.py:10
  (2 other events, 18.6 us)
Sparse Core Ops, SparseCore 0:
  629.0 151.6 reduce-scatter.3
